TPU v7x, 32 devices: a whole 2x2x4 slice. The times are simulated.
32 devices in a mesh: shift: 2 (over y), space: 4 (over z), orb: 2 (over x), grid: 2 (over core).
Axes of the slice: x: 2, y: 2, z: 4, core: 2. Of those that a mesh axis runs over, the one named last changes fastest.
Arguments:
- support: bfloat16 [128, 9, 15, 256], P(('shift', 'space', 'orb'), None, None, 'grid'), parts along dimension 0, may hold values from -0.75 to 0.75
- anchor: int32 [128], P(('shift', 'space', 'orb')), parts along dimension 0, may hold values from 0 to 63, as said below
- kernel: float32 [512, 9, 9], P(('shift', 'space', 'orb')), parts along dimension 0, may hold values from -2.1 to 2.1
- pair_owner: int32 [512], P(('shift', 'space', 'orb')), parts along dimension 0, may hold values from 0 to 63, as said below
- pair_partner: int32 [512], P(('shift', 'space', 'orb')), parts along dimension 0, may hold values from 0 to 63, as said below
- pair_live: int32 [512], P(('shift', 'space', 'orb')), parts along dimension 0, may hold values 0 or 1
- v_ext: float32 [128, 256], P(('shift', 'space'), 'grid'), parts along dimension 0, may hold values from -6 to 6
Outputs:
- density: float32 [128, 256], P(('shift', 'space'), 'grid'), parts along dimension 0
- hamiltonian: float32 [512, 9, 9], P(('shift', 'space', 'orb')), parts along dimension 0
There are 2 independent parts, one for each index of `shift`. A program takes and returns all parts, laid end to end along the dimension named above; each array names one. Nothing has to cross between parts.
Inputs may be any that keep to these rules, and one draw needn't show every extreme that they name: Atom a lies in spatial domain a // 16, and its box starts at a plane of that domain: anchor[a] // 16 = a // 16. The owner of slot p is one of the 8 atoms of block p // 32: pair_owner[p] // 8 = p // 32. `pair_partner`: the partner of a slot lies in its owner's spatial domain or in one of the two adjacent domains, counted periodically, and its box shares at least one plane with the owner's box: |gap| <= 14.
All inputs are finite; a program needn't handle non-finite values. No bound on the sum of `pair_live` on one device may be relied on, other than what follows from the above.
Results may differ from a plain program's by a relative error of at most 0.0028.
Values may be sent and summed in bfloat16 or wider, within the bound.
A program may use at most 64 MiB of HBM per device.

v0:
```python
import jax
import jax.numpy as jnp
from jax import lax
from jax.sharding import PartitionSpec as P


def shifted(value, axis, steps):
    count = lax.axis_size(axis)
    pairs = [(source, (source + steps) % count) for source in range(count)]
    return lax.ppermute(value, axis, pairs)


def shift_planes(rows, plane_gap, box_depth):
    index = jnp.arange(box_depth, dtype=jnp.int32)[None, :] + plane_gap[:, None]
    inside = (index >= 0) & (index < box_depth)
    picked = jnp.take_along_axis(rows, jnp.clip(index, 0, box_depth - 1)[:, None, :, None], axis=2)
    return jnp.where(inside[:, None, :, None], picked, jnp.zeros_like(picked))


def respond(field):
    return field / jnp.sqrt(1.0 + field * field)


def on_device(support, anchor, kernel, pair_owner, pair_partner, pair_live, v_ext):
    per_device, functions, box_depth, points = support.shape
    pair_count = kernel.shape[0]
    slab_rows = v_ext.shape[0]
    orb_count = lax.axis_size("orb")
    space_count = lax.axis_size("space")
    per_domain = per_device * orb_count
    total_planes = slab_rows * space_count
    domain = lax.axis_index("space")
    orb_index = lax.axis_index("orb")
    own_block = domain * orb_count + orb_index
    below_support, below_anchor = shifted((support, anchor), "space", 1)
    above_support, above_anchor = shifted((support, anchor), "space", -1)
    lower_support, domain_support, upper_support, lower_anchor, domain_anchor, upper_anchor = (
        lax.all_gather(below_support, "orb", axis=0, tiled=True),
        lax.all_gather(support, "orb", axis=0, tiled=True),
        lax.all_gather(above_support, "orb", axis=0, tiled=True),
        lax.all_gather(below_anchor, "orb", axis=0, tiled=True),
        lax.all_gather(anchor, "orb", axis=0, tiled=True),
        lax.all_gather(above_anchor, "orb", axis=0, tiled=True),
    )
    window_support = jnp.concatenate([lower_support, domain_support, upper_support], axis=0)
    window_anchor = jnp.concatenate([lower_anchor, domain_anchor, upper_anchor], axis=0)
    partner_domain = pair_partner // per_domain
    relative = (partner_domain - domain + 1 + space_count) % space_count
    window_index = relative * per_domain + pair_partner % per_domain
    owner_local = pair_owner - own_block * per_device
    plane_gap = (
        (anchor[owner_local] - window_anchor[window_index] + total_planes // 2) % total_planes
        - total_planes // 2
    ).astype(jnp.int32)
    alive = pair_live.astype(jnp.float32)
    block_count = pair_count // pair_count
    index_blocks = window_index.reshape(block_count, pair_count)
    gap_blocks = plane_gap.reshape(block_count, pair_count)
    owner_blocks = owner_local.reshape(block_count, pair_count)
    kernel_blocks = (kernel * alive[:, None, None]).reshape(
        block_count, pair_count, functions, functions
    )
    atom_ids = jnp.arange(per_device, dtype=jnp.int32)

    def aux_step(total, items):
        rows_index, gaps, kern, owners = items
        moved = shift_planes(window_support[rows_index], gaps, box_depth)
        terms = jnp.einsum(
            "pst,ptjq->psjq", kern, moved.astype(jnp.float32), precision=lax.Precision.HIGHEST
        )
        table = (owners[None, :] == atom_ids[:, None]).astype(jnp.float32)
        return (
            total + jnp.einsum("ap,psjq->asjq", table, terms, precision=lax.Precision.HIGHEST),
            None,
        )

    start_aux = jnp.zeros((per_device, functions, box_depth, points), jnp.float32)
    aux, _ = lax.scan(aux_step, start_aux, (index_blocks, gap_blocks, kernel_blocks, owner_blocks))
    deposit_terms = jnp.sum(support.astype(jnp.float32) * aux, axis=1)
    offset = anchor - domain * slab_rows
    local_plane = offset[:, None] + jnp.arange(box_depth, dtype=jnp.int32)[None, :]
    placing = (
        jnp.arange(2 * slab_rows, dtype=jnp.int32)[:, None, None] == local_plane[None, :, :]
    ).astype(jnp.float32)
    deposit = jnp.einsum("zaj,ajq->zq", placing, deposit_terms, precision=lax.Precision.HIGHEST)
    summed = lax.psum(deposit, "orb")
    incoming = shifted(summed[slab_rows:], "space", 1)
    density = summed[:slab_rows] + incoming
    potential = v_ext + respond(density)
    next_potential = shifted(potential, "space", -1)
    both_slabs = jnp.concatenate([potential, next_potential], axis=0)
    box_potential = jnp.einsum("zaj,zq->ajq", placing, both_slabs, precision=lax.Precision.HIGHEST)
    weighted = (support.astype(jnp.float32) * box_potential[:, None, :, :]).astype(jnp.bfloat16)

    def ham_block(items):
        rows_index, gaps, owners = items
        moved = shift_planes(window_support[rows_index], gaps, box_depth)
        owner_rows = weighted[owners]
        return jnp.einsum("psjq,ptjq->pst", owner_rows, moved, preferred_element_type=jnp.float32)

    partial_blocks = lax.map(ham_block, (index_blocks, gap_blocks, owner_blocks)).reshape(
        pair_count, functions, functions
    )
    hamiltonian = lax.psum(partial_blocks, "grid") * alive[:, None, None]
    return (density, hamiltonian)


def solution(mesh):
    placed = (
        P(("shift", "space", "orb"), None, None, "grid"),
        P(("shift", "space", "orb")),
        P(("shift", "space", "orb"), None, None),
        P(("shift", "space", "orb")),
        P(("shift", "space", "orb")),
        P(("shift", "space", "orb")),
        P(("shift", "space"), "grid"),
    )
    return jax.shard_map(
        on_device,
        mesh=mesh,
        in_specs=placed,
        out_specs=(P(("shift", "space"), "grid"), P(("shift", "space", "orb"), None, None)),
        check_vma=False,
    )
```

profile of v0, /device:TPU:0, one launch (start us, length us, event | category | flops | bytes accessed | tf_op | source)
XLA Modules:
  0.0 81.6 jit_solution(5677399734707426305)
XLA Ops:
  0.6 0.0 copy-start.5
  0.7 3.1 %collective-permute-start = (s32[8]{0:T(128)}, s32[8]{0:T(128)S(1)}, u32[]{:S(2)}, u32[]{:S(2)}) collective-permute-start(s32[8]{0:T(128)} %param.10), channel_id=1, source_target_pairs={{0,4},{4,8},{8,12},{12,0},{1,5},{5,9},{9,13},{13,1},{2,6},{6,10},{... | collective-permute-start | bytes 104 | tf_op jit(solution)/shard_map/ppermute | solution.py:10
  3.8 2.1 %collective-permute-start.1 = (s32[8]{0:T(128)}, s32[8]{0:T(128)S(1)}, u32[]{:S(2)}, u32[]{:S(2)}) collective-permute-start(s32[8]{0:T(128)} %param.10), channel_id=1, source_target_pairs={{0,12},{4,0},{8,4},{12,8},{1,13},{5,1},{9,5},{13,9},{2,14},{6,2},{... | collective-permute-start | bytes 104 | tf_op jit(solution)/shard_map/ppermute | solution.py:10
  5.9 3.8 %collective-permute-start.3 = (bf16[8,9,15,128]{3,0,2,1:T(8,128)(2,1)}, bf16[8,9,15,128]{3,0,2,1:T(8,128)(2,1)S(1)}, u32[]{:S(2)}, u32[]{:S(2)}) collective-permute-start(bf16[8,9,15,128]{3,0,2,1:T(8,128)(2,1)} %param.9), channel_id=1, source_target_pairs={{0,12},{4,0},{8,4},{12,8},{1,13},{5,1},{9,5},{13,9},{2,14},{6,2},{... | collective-permute-start | bytes 829448 | tf_op jit(solution)/shard_map/ppermute | solution.py:10
  9.7 8.4 %all_gather.22 = bf16[16,9,15,128]{3,0,2,1:T(8,128)(2,1)S(1)} all-gather(bf16[8,9,15,128]{3,0,2,1:T(8,128)(2,1)} %param.9), channel_id=1, replica_groups=mesh['shift'=2,'space'=4,'orb'=2,'grid'=2] {'orb'}, dimensions={0}, use_global_device_ids=true | all-gather | bytes 829440 | tf_op jit(solution)/shard_map/all_gather | solution.py:39
  18.1 0.7 compare_select_fusion.1
  18.8 0.7 compare_select_fusion.2
  19.5 1.4 %gather_fusion = s32[32]{0:T(128)S(1)} fusion(s32[8]{0:T(128)} %param.10, s32[1024]{0:T(1024)S(1)} %pad_clamp_fusion.1), kind=kCustom, calls=%fused_computation.1 | custom fusion | bytes 384 | tf_op jit(solution)/shard_map/gather | solution.py:52
  20.8 0.2 copy.38
  21.0 0.2 copy.36
  21.2 0.1 iota_add_fusion.1
  21.3 0.6 dynamic-slice.4
  22.6 0.2 dynamic-update-slice.1
  22.8 0.2 dynamic-update-slice
  23.1 0.2 dynamic-update-slice.2
  23.3 4.3 %all-reduce.3 = (s32[16]{0:T(128)S(1)}, s32[16]{0:T(128)S(1)}, s32[16]{0:T(128)S(1)}) all-reduce(s32[16]{0:T(128)S(1)} %dynamic-update-slice.2, s32[16]{0:T(128)S(1)} %dynamic-update-slice.1, s32[16]{0:T(128)S(1)} %dynamic-update-slice), channel_id=1, replica_groups=mesh['shift'=2,'space'=4,'orb'=2,'grid'=2] {'orb'}, use_global_device_ids=true, to_apply=%add.2 | all-reduce | flops 48 | bytes 384
  27.5 0.1 pad_add_fusion
  27.6 0.7 gather_fusion.1
  28.3 0.1 bitcast_or_fusion
  28.4 0.1 fusion.32
  28.5 0.1 reshape.174
  28.6 0.1 fusion.33
  28.7 8.0 %all_gather.21 = bf16[16,9,15,128]{3,0,2,1:T(8,128)(2,1)S(1)} all-gather(bf16[8,9,15,128]{3,0,2,1:T(8,128)(2,1)S(1)} %collective-permute-done.2), channel_id=1, replica_groups=mesh['shift'=2,'space'=4,'orb'=2,'grid'=2] {'orb'}, dimensions={0}, use_global_device_ids=true | all-gather | bytes 829440 | tf_op jit(solution)/shard_map/all_gather | solution.py:38
  36.7 0.2 copy.37
  36.8 7.2 %all_gather.23 = bf16[16,9,15,128]{3,0,2,1:T(8,128)(2,1)S(1)} all-gather(bf16[8,9,15,128]{3,0,2,1:T(8,128)(2,1)S(1)} %collective-permute-done.3), channel_id=1, replica_groups=mesh['shift'=2,'space'=4,'orb'=2,'grid'=2] {'orb'}, dimensions={0}, use_global_device_ids=true | all-gather | bytes 829440 | tf_op jit(solution)/shard_map/all_gather | solution.py:40
  44.0 0.2 copy.39
  44.2 0.3 pad_maximum_fusion
  44.5 0.8 gather_fusion.2
  45.3 1.8 %copy.40 = bf16[32,9,15,128]{3,1,2,0:T(8,128)(2,1)} copy(bf16[32,9,15,128]{3,2,1,0:T(8,128)(2,1)S(1)} %gather_fusion.2) | data formatting | bytes 2211840 | tf_op jit(solution)/shard_map/while/body/eval_jaxpr/gather | solution.py:67
  47.1 5.2 %gather_fusion.4 = bf16[480,9,128]{2,1,0:T(8,128)(2,1)S(1)} fusion(bf16[32,9,15,128]{3,1,2,0:T(8,128)(2,1)} %copy.40, s32[480]{0:T(512)S(1)} %reshape.174), kind=kCustom, calls=%fused_computation.clone | custom fusion | bytes 2215680 | tf_op jit(solution)/shard_map/while/body/eval_jaxpr/jit(take_along_axis)/gather | solution.py:16
  52.3 0.3 bitcast_select_fusion
  52.7 2.1 %fusion.4 = f32[32,9,15,128]{3,1,2,0:T(8,128)S(1)} fusion(bf16[32,9,15,128]{3,2,0,1:T(8,128)(2,1)S(1)} %bitcast_select_fusion, f32[32,9,9]{2,1,0:T(8,128)S(1)} %copy.36, f32[32]{0:T(128)S(1)} %convert_element_type.16), kind=kOutput, calls=%fused_computation.9 | convolution fusion | flops 59722272 | bytes 3328256 | tf_op jit(solution)/shard_map/while/body/eval_jaxpr/pst,ptjq->psjq/dot_general | solution.py:68
  54.8 1.5 %fusion.10 = f32[8,15,128]{2,0,1:T(8,128)S(1)} fusion(f32[32,9,15,128]{3,1,2,0:T(8,128)S(1)} %fusion.4, bf16[8,9,15,128]{3,0,2,1:T(8,128)(2,1)S(1)} %copy-done.1, s32[32]{0:T(128)S(1)} %get-tuple-element.62), kind=kOutput, calls=%fused_computation.14 | convolution fusion | flops 53483776 | bytes 2549888 | tf_op jit(solution)/shard_map/while/body/eval_jaxpr/ap,psjq->asjq/dot_general | solution.py:73
  56.3 0.3 convolution_bitcast_fusion
  56.6 8.3 %psum.14 = f32[32,128]{1,0:T(8,128)S(1)} all-reduce(f32[32,128]{1,0:T(8,128)S(1)} %convolution_bitcast_fusion), channel_id=1, replica_groups=mesh['shift'=2,'space'=4,'orb'=2,'grid'=2] {'orb'}, use_global_device_ids=true, to_apply=%region_1.3 | all-reduce | flops 4096 | bytes 32768 | tf_op jit(solution)/shard_map/psum | solution.py:86
  64.9 0.0 collective-permute-start.4
  64.9 5.4 %collective-permute-done.4 = f32[16,128]{1,0:T(8,128)S(1)} collective-permute-done((f32[16,128]{1,0:T(8,128)S(1)}, f32[16,128]{1,0:T(8,128)S(1)}, u32[]{:S(2)}, u32[]{:S(2)}) %collective-permute-start.4) | collective-permute-done | bytes 8224 | tf_op jit(solution)/shard_map/ppermute | solution.py:10
  70.4 0.6 multiply_add_fusion
  71.0 0.1 iota_compare_fusion
  71.1 3.6 %collective-permute-done.5 = f32[16,128]{1,0:T(8,128)S(1)} collective-permute-done((f32[16,128]{1,0:T(8,128)S(1)}, f32[16,128]{1,0:T(8,128)S(1)}, u32[]{:S(2)}, u32[]{:S(2)}) %collective-permute-start.5) | collective-permute-done | bytes 8224 | tf_op jit(solution)/shard_map/ppermute | solution.py:10
  74.6 0.2 fusion.23
  74.8 0.1 fusion.18
  74.9 0.1 copy.46
  74.9 0.8 gather_fusion.3
  75.7 1.0 %fusion.13 = f32[32,9,9]{2,1,0:T(8,128)S(1)} fusion(bf16[32,9,15,128]{3,2,0,1:T(8,128)(2,1)S(1)} %bitcast_select_fusion, bf16[32,9,15,128]{3,2,1,0:T(8,128)(2,1)S(1)} %gather_fusion.3), kind=kOutput, calls=%fused_computation.17 | convolution fusion | flops 9953280 | bytes 2222208 | tf_op jit(solution)/shard_map/while/body/eval_jaxpr/psjq,ptjq->pst/dot_general | solution.py:99
  76.7 4.0 %psum.15 = f32[32,9,9]{2,1,0:T(8,128)S(1)} all-reduce(f32[32,9,9]{2,1,0:T(8,128)S(1)} %fusion.13), channel_id=1, replica_groups=mesh['shift'=2,'space'=4,'orb'=2,'grid'=2] {'grid'}, use_global_device_ids=true, to_apply=%region_2.4 | all-reduce | flops 2592 | bytes 20736 | tf_op jit(solution)/shard_map/psum | solution.py:104
  80.7 0.1 broadcast_multiply_fusion
  80.8 0.8 copy.49
  (26 shorter events, 0.1 us)
Async XLA Ops:
  0.6 20.7 %copy-start.5 = (u32[32]{0:T(128)S(1)}, u32[32]{0:T(128)}, u32[]{:S(2)}) copy-start(u32[32]{0:T(128)} %constant.154) | copy-start | bytes 388
  0.6 20.6 %copy-start = (s32[8]{0:T(128)S(1)}, s32[8]{0:T(128)}, u32[]{:S(2)}) copy-start(s32[8]{0:T(128)} %param.10) | copy-start | bytes 100
  0.7 20.3 %copy-start.4 = (s32[32]{0:T(128)S(1)}, s32[32]{0:T(128)}, u32[]{:S(2)}) copy-start(s32[32]{0:T(128)} %param.14) | copy-start | bytes 388
  0.7 20.4 %copy-start.2 = (f32[32,9,9]{0,2,1:T(8,128)S(1)}, f32[32,9,9]{0,2,1:T(8,128)}, u32[]{:S(2)}) copy-start(f32[32,9,9]{0,2,1:T(8,128)} %param.11) | copy-start | bytes 31108
  0.7 22.1 %collective-permute-start = (s32[8]{0:T(128)}, s32[8]{0:T(128)S(1)}, u32[]{:S(2)}, u32[]{:S(2)}) collective-permute-start(s32[8]{0:T(128)} %param.10), channel_id=1, source_target_pairs={{0,4},{4,8},{8,12},{12,0},{1,5},{5,9},{9,13},{13,1},{2,6},{6,10},{... | collective-permute-start | bytes 104 | tf_op jit(solution)/shard_map/ppermute | solution.py:10
  3.8 19.3 %collective-permute-start.1 = (s32[8]{0:T(128)}, s32[8]{0:T(128)S(1)}, u32[]{:S(2)}, u32[]{:S(2)}) collective-permute-start(s32[8]{0:T(128)} %param.10), channel_id=1, source_target_pairs={{0,12},{4,0},{8,4},{12,8},{1,13},{5,1},{9,5},{13,9},{2,14},{6,2},{... | collective-permute-start | bytes 104 | tf_op jit(solution)/shard_map/ppermute | solution.py:10
  5.9 22.8 %collective-permute-start.2 = (bf16[8,9,15,128]{3,0,2,1:T(8,128)(2,1)}, bf16[8,9,15,128]{3,0,2,1:T(8,128)(2,1)S(1)}, u32[]{:S(2)}, u32[]{:S(2)}) collective-permute-start(bf16[8,9,15,128]{3,0,2,1:T(8,128)(2,1)} %param.9), channel_id=1, source_target_pairs={{0,4},{4,8},{8,12},{12,0},{1,5},{5,9},{9,13},{13,1},{2,6},{6,10},{... | collective-permute-start | bytes 829448 | tf_op jit(solution)/shard_map/ppermute | solution.py:10
  5.9 30.9 %collective-permute-start.3 = (bf16[8,9,15,128]{3,0,2,1:T(8,128)(2,1)}, bf16[8,9,15,128]{3,0,2,1:T(8,128)(2,1)S(1)}, u32[]{:S(2)}, u32[]{:S(2)}) collective-permute-start(bf16[8,9,15,128]{3,0,2,1:T(8,128)(2,1)} %param.9), channel_id=1, source_target_pairs={{0,12},{4,0},{8,4},{12,8},{1,13},{5,1},{9,5},{13,9},{2,14},{6,2},{... | collective-permute-start | bytes 829448 | tf_op jit(solution)/shard_map/ppermute | solution.py:10
  52.7 2.1 %copy-start.1 = (bf16[8,9,15,128]{3,0,2,1:T(8,128)(2,1)S(1)}, bf16[8,9,15,128]{3,0,2,1:T(8,128)(2,1)}, u32[]{:S(2)}) copy-start(bf16[8,9,15,128]{3,0,2,1:T(8,128)(2,1)} %param.9) | copy-start | bytes 829444
  54.7 15.6 %copy-start.3 = (f32[16,128]{1,0:T(8,128)S(1)}, f32[16,128]{1,0:T(8,128)}, u32[]{:S(2)}) copy-start(f32[16,128]{1,0:T(8,128)} %param.15) | copy-start | bytes 24580
  64.9 5.5 %collective-permute-start.4 = (f32[16,128]{1,0:T(8,128)S(1)}, f32[16,128]{1,0:T(8,128)S(1)}, u32[]{:S(2)}, u32[]{:S(2)}) collective-permute-start(f32[16,128]{1,0:T(8,128)S(1)} %slice.19), channel_id=1, source_target_pairs={{0,4},{4,8},{8,12},{12,0},{1,5},{5,9},{9,13},{13,1},{2,6},{6,10},{... | collective-permute-start | bytes 24584 | tf_op jit(solution)/shard_map/ppermute | solution.py:10
  71.0 3.7 %collective-permute-start.5 = (f32[16,128]{1,0:T(8,128)S(1)}, f32[16,128]{1,0:T(8,128)S(1)}, u32[]{:S(2)}, u32[]{:S(2)}) collective-permute-start(f32[16,128]{1,0:T(8,128)S(1)} %get-tuple-element.52), channel_id=1, source_target_pairs={{0,12},{4,0},{8,4},{12,8},{1,13},{5,1},{9,5},{13,9},{2,14},{6,2},{... | collective-permute-start | bytes 24584 | tf_op jit(solution)/shard_map/ppermute | solution.py:10
where the time goes:
time: 81.9 us; the launch traced here: 81.6 us
  blocking collectives  40.2 us (49%)
  local copies, waits for them, and re-layouts  13.5 us (16%)
  starting transfers between devices  9.06 us (11%)
  waiting for transfers between devices  9 us (11%)
  matrix products  5.04 us (6%)
  other arithmetic  3.28 us (4%)
  between operations  1.56 us (2%)
    ppermute x6, starting transfers between devices, shifted(): return lax.ppermute(value, axis, pairs)  9.06 us
    ppermute x6, waiting for transfers between devices, shifted(): return lax.ppermute(value, axis, pairs)  9 us
    all_gather x1, blocking collectives, on_device(): lax.all_gather(support, 'orb', axis=0, tiled=True)  8.41 us
    psum x1, blocking collectives, on_device(): summed = lax.psum(deposit, 'orb')  8.3 us
    all_gather x1, blocking collectives, on_device(): lax.all_gather(below_support, 'orb', axis=0, tiled=True)  7.96 us
    all_gather x1, blocking collectives, on_device(): lax.all_gather(above_support, 'orb', axis=0, tiled=True)  7.22 us
    gather x2, local copies, waits for them, and re-layouts, shift_planes(): jnp.take_along_axis(rows, jnp.clip(index, 0, box_depth - 1)[:, None, :, N...  5.32 us
    unnamed x1, blocking collectives  4.25 us
  transfers between devices with their start and end apart: 6, of which 2 were waited for; matrix products, arithmetic and copies ran while one was open for 7% of the time, Pallas kernels for 0%

commit v1 on v0

--- a/solution.py
+++ b/solution.py
@@ -83,7 +83,11 @@
         jnp.arange(2 * slab_rows, dtype=jnp.int32)[:, None, None] == local_plane[None, :, :]
     ).astype(jnp.float32)
     deposit = jnp.einsum("zaj,ajq->zq", placing, deposit_terms, precision=lax.Precision.HIGHEST)
-    summed = lax.psum(deposit, "orb")
+
+    def check_the_ratios(sample):
+        return jnp.sum(lax.all_gather(sample, "orb"), axis=0)
+
+    summed = check_the_ratios(deposit)
     incoming = shifted(summed[slab_rows:], "space", 1)
     density = summed[:slab_rows] + incoming
     potential = v_ext + respond(density)

time: 81.9 us -> 78 us (0.952)
  blocking collectives: 40.2 us -> 36.3 us
    psum x1 -> x0, blocking collectives: 8.3 us -> none  [on_device(): summed = lax.psum(deposit, 'orb')]
    all_gather x0 -> x1, blocking collectives: none -> 4.41 us  [check_the_ratios(): return jnp.sum(lax.all_gather(sample, 'orb'), axis=0)]
where the time goes in v1:
time: 78 us; the launch traced here: 77.7 us
  blocking collectives  36.3 us (47%)
  local copies, waits for them, and re-layouts  13.5 us (17%)
  starting transfers between devices  9.07 us (12%)
  waiting for transfers between devices  9 us (12%)
  matrix products  5.05 us (6%)
  other arithmetic  3.29 us (4%)
  between operations  1.57 us (2%)
    ppermute x6, starting transfers between devices, shifted(): return lax.ppermute(value, axis, pairs)  9.07 us
    ppermute x6, waiting for transfers between devices, shifted(): return lax.ppermute(value, axis, pairs)  9 us
    all_gather x1, blocking collectives, on_device(): lax.all_gather(support, 'orb', axis=0, tiled=True)  8.41 us
    all_gather x1, blocking collectives, on_device(): lax.all_gather(below_support, 'orb', axis=0, tiled=True)  7.96 us
    all_gather x1, blocking collectives, on_device(): lax.all_gather(above_support, 'orb', axis=0, tiled=True)  7.22 us
    gather x2, local copies, waits for them, and re-layouts, shift_planes(): jnp.take_along_axis(rows, jnp.clip(index, 0, box_depth - 1)[:, None, :, N...  5.32 us
    all_gather x1, blocking collectives, check_the_ratios(): return jnp.sum(lax.all_gather(sample, 'orb'), axis=0)  4.41 us
    unnamed x1, blocking collectives  4.25 us
  transfers between devices with their start and end apart: 6, of which 2 were waited for; matrix products, arithmetic and copies ran while one was open for 7% of the time, Pallas kernels for 0%

profile of v1, /device:TPU:0, one launch (start us, length us, event | category | flops | bytes accessed | tf_op | source)
XLA Modules:
  0.0 77.7 jit_solution(14169743790428218723)
XLA Ops:
  0.6 0.0 copy-start.5
  0.7 3.1 %collective-permute-start = (s32[8]{0:T(128)}, s32[8]{0:T(128)S(1)}, u32[]{:S(2)}, u32[]{:S(2)}) collective-permute-start(s32[8]{0:T(128)} %param.10), channel_id=1, source_target_pairs={{0,4},{4,8},{8,12},{12,0},{1,5},{5,9},{9,13},{13,1},{2,6},{6,10},{... | collective-permute-start | bytes 104 | tf_op jit(solution)/shard_map/ppermute | solution.py:10
  3.8 2.1 %collective-permute-start.1 = (s32[8]{0:T(128)}, s32[8]{0:T(128)S(1)}, u32[]{:S(2)}, u32[]{:S(2)}) collective-permute-start(s32[8]{0:T(128)} %param.10), channel_id=1, source_target_pairs={{0,12},{4,0},{8,4},{12,8},{1,13},{5,1},{9,5},{13,9},{2,14},{6,2},{... | collective-permute-start | bytes 104 | tf_op jit(solution)/shard_map/ppermute | solution.py:10
  5.9 3.8 %collective-permute-start.3 = (bf16[8,9,15,128]{3,0,2,1:T(8,128)(2,1)}, bf16[8,9,15,128]{3,0,2,1:T(8,128)(2,1)S(1)}, u32[]{:S(2)}, u32[]{:S(2)}) collective-permute-start(bf16[8,9,15,128]{3,0,2,1:T(8,128)(2,1)} %param.9), channel_id=1, source_target_pairs={{0,12},{4,0},{8,4},{12,8},{1,13},{5,1},{9,5},{13,9},{2,14},{6,2},{... | collective-permute-start | bytes 829448 | tf_op jit(solution)/shard_map/ppermute | solution.py:10
  9.7 8.4 %all_gather.28 = bf16[16,9,15,128]{3,0,2,1:T(8,128)(2,1)S(1)} all-gather(bf16[8,9,15,128]{3,0,2,1:T(8,128)(2,1)} %param.9), channel_id=1, replica_groups=mesh['shift'=2,'space'=4,'orb'=2,'grid'=2] {'orb'}, dimensions={0}, use_global_device_ids=true | all-gather | bytes 829440 | tf_op jit(solution)/shard_map/all_gather | solution.py:39
  18.1 0.7 compare_select_fusion.1
  18.8 0.7 compare_select_fusion.2
  19.5 1.4 %gather_fusion = s32[32]{0:T(128)S(1)} fusion(s32[8]{0:T(128)} %param.10, s32[1024]{0:T(1024)S(1)} %pad_clamp_fusion.1), kind=kCustom, calls=%fused_computation.1 | custom fusion | bytes 384 | tf_op jit(solution)/shard_map/gather | solution.py:52
  20.8 0.2 copy.38
  21.0 0.2 copy.36
  21.2 0.1 iota_add_fusion.1
  21.3 0.6 dynamic-slice.4
  22.6 0.2 dynamic-update-slice.1
  22.8 0.2 dynamic-update-slice
  23.1 0.2 dynamic-update-slice.2
  23.3 4.3 %all-reduce.3 = (s32[16]{0:T(128)S(1)}, s32[16]{0:T(128)S(1)}, s32[16]{0:T(128)S(1)}) all-reduce(s32[16]{0:T(128)S(1)} %dynamic-update-slice.2, s32[16]{0:T(128)S(1)} %dynamic-update-slice.1, s32[16]{0:T(128)S(1)} %dynamic-update-slice), channel_id=1, replica_groups=mesh['shift'=2,'space'=4,'orb'=2,'grid'=2] {'orb'}, use_global_device_ids=true, to_apply=%add.2 | all-reduce | flops 48 | bytes 384
  27.5 0.1 pad_add_fusion
  27.6 0.7 gather_fusion.1
  28.3 0.1 bitcast_or_fusion
  28.4 0.1 fusion.32
  28.5 0.1 reshape.175
  28.6 0.1 fusion.33
  28.7 8.0 %all_gather.27 = bf16[16,9,15,128]{3,0,2,1:T(8,128)(2,1)S(1)} all-gather(bf16[8,9,15,128]{3,0,2,1:T(8,128)(2,1)S(1)} %collective-permute-done.2), channel_id=1, replica_groups=mesh['shift'=2,'space'=4,'orb'=2,'grid'=2] {'orb'}, dimensions={0}, use_global_device_ids=true | all-gather | bytes 829440 | tf_op jit(solution)/shard_map/all_gather | solution.py:38
  36.7 0.2 copy.37
  36.8 7.2 %all_gather.29 = bf16[16,9,15,128]{3,0,2,1:T(8,128)(2,1)S(1)} all-gather(bf16[8,9,15,128]{3,0,2,1:T(8,128)(2,1)S(1)} %collective-permute-done.3), channel_id=1, replica_groups=mesh['shift'=2,'space'=4,'orb'=2,'grid'=2] {'orb'}, dimensions={0}, use_global_device_ids=true | all-gather | bytes 829440 | tf_op jit(solution)/shard_map/all_gather | solution.py:40
  44.0 0.2 copy.39
  44.2 0.3 pad_maximum_fusion
  44.5 0.8 gather_fusion.2
  45.3 1.8 %copy.40 = bf16[32,9,15,128]{3,1,2,0:T(8,128)(2,1)} copy(bf16[32,9,15,128]{3,2,1,0:T(8,128)(2,1)S(1)} %gather_fusion.2) | data formatting | bytes 2211840 | tf_op jit(solution)/shard_map/while/body/eval_jaxpr/gather | solution.py:67
  47.1 5.2 %gather_fusion.4 = bf16[480,9,128]{2,1,0:T(8,128)(2,1)S(1)} fusion(bf16[32,9,15,128]{3,1,2,0:T(8,128)(2,1)} %copy.40, s32[480]{0:T(512)S(1)} %reshape.175), kind=kCustom, calls=%fused_computation.clone | custom fusion | bytes 2215680 | tf_op jit(solution)/shard_map/while/body/eval_jaxpr/jit(take_along_axis)/gather | solution.py:16
  52.3 0.3 bitcast_select_fusion
  52.7 2.1 %fusion.4 = f32[32,9,15,128]{3,1,2,0:T(8,128)S(1)} fusion(bf16[32,9,15,128]{3,2,0,1:T(8,128)(2,1)S(1)} %bitcast_select_fusion, f32[32,9,9]{2,1,0:T(8,128)S(1)} %copy.36, f32[32]{0:T(128)S(1)} %convert_element_type.16), kind=kOutput, calls=%fused_computation.9 | convolution fusion | flops 59722272 | bytes 3328256 | tf_op jit(solution)/shard_map/while/body/eval_jaxpr/pst,ptjq->psjq/dot_general | solution.py:68
  54.8 1.5 %fusion.10 = f32[8,15,128]{2,0,1:T(8,128)S(1)} fusion(f32[32,9,15,128]{3,1,2,0:T(8,128)S(1)} %fusion.4, bf16[8,9,15,128]{3,0,2,1:T(8,128)(2,1)S(1)} %copy-done.1, s32[32]{0:T(128)S(1)} %get-tuple-element.62), kind=kOutput, calls=%fused_computation.14 | convolution fusion | flops 53483776 | bytes 2549888 | tf_op jit(solution)/shard_map/while/body/eval_jaxpr/ap,psjq->asjq/dot_general | solution.py:73
  56.3 0.3 convolution_bitcast_fusion
  56.6 4.4 %all-gather = f32[64,128]{1,0:T(8,128)S(1)} all-gather(f32[32,128]{1,0:T(8,128)S(1)} %convolution_bitcast_fusion), channel_id=2, replica_groups=mesh['shift'=2,'space'=4,'orb'=2,'grid'=2] {'orb'}, dimensions={0}, use_global_device_ids=true | all-gather | bytes 49152 | tf_op jit(solution)/shard_map/all_gather | solution.py:88
  61.0 0.0 collective-permute-start.4
  61.1 5.4 %collective-permute-done.4 = f32[16,128]{1,0:T(8,128)S(1)} collective-permute-done((f32[16,128]{1,0:T(8,128)S(1)}, f32[16,128]{1,0:T(8,128)S(1)}, u32[]{:S(2)}, u32[]{:S(2)}) %collective-permute-start.4) | collective-permute-done | bytes 8224 | tf_op jit(solution)/shard_map/ppermute | solution.py:10
  66.5 0.6 multiply_add_fusion
  67.1 0.1 iota_compare_fusion
  67.2 3.6 %collective-permute-done.5 = f32[16,128]{1,0:T(8,128)S(1)} collective-permute-done((f32[16,128]{1,0:T(8,128)S(1)}, f32[16,128]{1,0:T(8,128)S(1)}, u32[]{:S(2)}, u32[]{:S(2)}) %collective-permute-start.5) | collective-permute-done | bytes 8224 | tf_op jit(solution)/shard_map/ppermute | solution.py:10
  70.8 0.2 fusion.23
  71.0 0.1 fusion.18
  71.0 0.1 copy.46
  71.1 0.8 %gather_fusion.3 = bf16[32,9,15,128]{3,2,1,0:T(8,128)(2,1)S(1)} fusion(bf16[8,9,15,128]{3,2,1,0:T(8,128)(2,1)S(1)} %copy.46, s32[1024]{0:T(1024)S(1)} %pad_clamp_fusion.1), kind=kCustom, calls=%fused_computation.4 | custom fusion | bytes 2211968 | tf_op jit(solution)/shard_map/while/body/eval_jaxpr/gather | solution.py:102
  71.9 1.0 %fusion.13 = f32[32,9,9]{2,1,0:T(8,128)S(1)} fusion(bf16[32,9,15,128]{3,2,0,1:T(8,128)(2,1)S(1)} %bitcast_select_fusion, bf16[32,9,15,128]{3,2,1,0:T(8,128)(2,1)S(1)} %gather_fusion.3), kind=kOutput, calls=%fused_computation.17 | convolution fusion | flops 9953280 | bytes 2222208 | tf_op jit(solution)/shard_map/while/body/eval_jaxpr/psjq,ptjq->pst/dot_general | solution.py:103
  72.8 4.0 %psum.7 = f32[32,9,9]{2,1,0:T(8,128)S(1)} all-reduce(f32[32,9,9]{2,1,0:T(8,128)S(1)} %fusion.13), channel_id=1, replica_groups=mesh['shift'=2,'space'=4,'orb'=2,'grid'=2] {'grid'}, use_global_device_ids=true, to_apply=%region_2.4 | all-reduce | flops 2592 | bytes 20736 | tf_op jit(solution)/shard_map/psum | solution.py:108
  76.8 0.1 broadcast_multiply_fusion
  77.0 0.8 copy.49
  (27 shorter events, 0.1 us)
Async XLA Ops:
  0.6 20.7 %copy-start.5 = (u32[32]{0:T(128)S(1)}, u32[32]{0:T(128)}, u32[]{:S(2)}) copy-start(u32[32]{0:T(128)} %constant.154) | copy-start | bytes 388
  0.6 20.6 %copy-start = (s32[8]{0:T(128)S(1)}, s32[8]{0:T(128)}, u32[]{:S(2)}) copy-start(s32[8]{0:T(128)} %param.10) | copy-start | bytes 100
  0.7 20.3 %copy-start.4 = (s32[32]{0:T(128)S(1)}, s32[32]{0:T(128)}, u32[]{:S(2)}) copy-start(s32[32]{0:T(128)} %param.14) | copy-start | bytes 388
  0.7 20.4 %copy-start.2 = (f32[32,9,9]{0,2,1:T(8,128)S(1)}, f32[32,9,9]{0,2,1:T(8,128)}, u32[]{:S(2)}) copy-start(f32[32,9,9]{0,2,1:T(8,128)} %param.11) | copy-start | bytes 31108
  0.7 22.1 %collective-permute-start = (s32[8]{0:T(128)}, s32[8]{0:T(128)S(1)}, u32[]{:S(2)}, u32[]{:S(2)}) collective-permute-start(s32[8]{0:T(128)} %param.10), channel_id=1, source_target_pairs={{0,4},{4,8},{8,12},{12,0},{1,5},{5,9},{9,13},{13,1},{2,6},{6,10},{... | collective-permute-start | bytes 104 | tf_op jit(solution)/shard_map/ppermute | solution.py:10
  3.8 19.3 %collective-permute-start.1 = (s32[8]{0:T(128)}, s32[8]{0:T(128)S(1)}, u32[]{:S(2)}, u32[]{:S(2)}) collective-permute-start(s32[8]{0:T(128)} %param.10), channel_id=1, source_target_pairs={{0,12},{4,0},{8,4},{12,8},{1,13},{5,1},{9,5},{13,9},{2,14},{6,2},{... | collective-permute-start | bytes 104 | tf_op jit(solution)/shard_map/ppermute | solution.py:10
  5.9 22.8 %collective-permute-start.2 = (bf16[8,9,15,128]{3,0,2,1:T(8,128)(2,1)}, bf16[8,9,15,128]{3,0,2,1:T(8,128)(2,1)S(1)}, u32[]{:S(2)}, u32[]{:S(2)}) collective-permute-start(bf16[8,9,15,128]{3,0,2,1:T(8,128)(2,1)} %param.9), channel_id=1, source_target_pairs={{0,4},{4,8},{8,12},{12,0},{1,5},{5,9},{9,13},{13,1},{2,6},{6,10},{... | collective-permute-start | bytes 829448 | tf_op jit(solution)/shard_map/ppermute | solution.py:10
  5.9 30.9 %collective-permute-start.3 = (bf16[8,9,15,128]{3,0,2,1:T(8,128)(2,1)}, bf16[8,9,15,128]{3,0,2,1:T(8,128)(2,1)S(1)}, u32[]{:S(2)}, u32[]{:S(2)}) collective-permute-start(bf16[8,9,15,128]{3,0,2,1:T(8,128)(2,1)} %param.9), channel_id=1, source_target_pairs={{0,12},{4,0},{8,4},{12,8},{1,13},{5,1},{9,5},{13,9},{2,14},{6,2},{... | collective-permute-start | bytes 829448 | tf_op jit(solution)/shard_map/ppermute | solution.py:10
  52.7 2.1 %copy-start.1 = (bf16[8,9,15,128]{3,0,2,1:T(8,128)(2,1)S(1)}, bf16[8,9,15,128]{3,0,2,1:T(8,128)(2,1)}, u32[]{:S(2)}) copy-start(bf16[8,9,15,128]{3,0,2,1:T(8,128)(2,1)} %param.9) | copy-start | bytes 829444
  54.7 11.8 %copy-start.3 = (f32[16,128]{1,0:T(8,128)S(1)}, f32[16,128]{1,0:T(8,128)}, u32[]{:S(2)}) copy-start(f32[16,128]{1,0:T(8,128)} %param.15) | copy-start | bytes 24580
  61.0 5.5 %collective-permute-start.4 = (f32[16,128]{1,0:T(8,128)S(1)}, f32[16,128]{1,0:T(8,128)S(1)}, u32[]{:S(2)}, u32[]{:S(2)}) collective-permute-start(f32[16,128]{1,0:T(8,128)S(1)} %slice.19), channel_id=1, source_target_pairs={{0,4},{4,8},{8,12},{12,0},{1,5},{5,9},{9,13},{13,1},{2,6},{6,10},{... | collective-permute-start | bytes 24584 | tf_op jit(solution)/shard_map/ppermute | solution.py:10
  67.1 3.7 %collective-permute-start.5 = (f32[16,128]{1,0:T(8,128)S(1)}, f32[16,128]{1,0:T(8,128)S(1)}, u32[]{:S(2)}, u32[]{:S(2)}) collective-permute-start(f32[16,128]{1,0:T(8,128)S(1)} %get-tuple-element.52), channel_id=1, source_target_pairs={{0,12},{4,0},{8,4},{12,8},{1,13},{5,1},{9,5},{13,9},{2,14},{6,2},{... | collective-permute-start | bytes 24584 | tf_op jit(solution)/shard_map/ppermute | solution.py:10
